TPU v7x, 32 devices: a whole 2x2x4 slice. The times are simulated.
32 devices in a mesh: tm: 8 (over y, x, core), space: 4 (over z).
Axes of the slice: x: 2, y: 2, z: 4, core: 2. Of those that a mesh axis runs over, the one named last changes fastest.
Arguments:
- adjoint_iterate: float32 [64, 16, 32, 128], P('tm', None, 'space'), may hold values from -6 to 6
- innovations: float32 [64, 16, 512], P('tm', None, 'space'), may hold values from -6 to 6
- station_cells: int32 [64, 512], P('tm', 'space'), may hold values from 0 to 1023
- diffusivity: float32 [16, 32, 128], P(None, 'space'), may hold values from 0.01 to 0.08
- wind_x: float32 [16, 32, 128], P(None, 'space'), may hold values from -0.2 to 0.2
- wind_y: float32 [16, 32, 128], P(None, 'space'), may hold values from -0.2 to 0.2
- vertical_mixing: float32 [16, 32, 128], P(None, 'space'), may hold values from 0.01 to 0.1
Outputs:
- updated_iterate: float32 [64, 16, 32, 128], P('tm', None, 'space')
Inputs may be any that keep to these rules, and one draw needn't show every extreme that they name: `station_cells`: A station's column within its tile of 8 x 128 columns is numbered x * 128 + y; several stations may share a column.
All inputs are finite; a program needn't handle non-finite values.
Results may differ from a plain program's by a relative error of at most 0.0003.
Values sent between devices are 32-bit elements; how exact they have to be, the bound alone decides.
No kernel may reach another device: no remote copies, remote signals or barrier semaphores. Data moves between devices by JAX's collectives and lax.ppermute only.
A program may use at most 64 MiB of HBM per device.

v0:
```python
import math
import jax
import jax.numpy as jnp
from jax import lax
from jax.sharding import PartitionSpec as P

LEV = 16
TX = 8
NY = 128
STEPS_DEV = 8
INNER = 4
circ_alpha = 0.1


def from_behind(value, axis, steps):
    count = lax.axis_size(axis)
    leading, last = (max(0, -steps), min(count, count - steps))
    return lax.ppermute(value, axis, [(source, source + steps) for source in range(leading, last)])


def with_halo(cells, sides, width):
    for axis, dim in sides:
        count = lax.axis_size(axis)
        ends = count - 1
        head = lax.slice_in_dim(cells, 0, width, axis=dim)
        tail = lax.slice_in_dim(cells, cells.shape[dim] - width, cells.shape[dim], axis=dim)
        cells = jnp.concatenate(
            [
                lax.ppermute(tail, axis, [(i, (i + 1) % count) for i in range(ends)]),
                cells,
                lax.ppermute(head, axis, [((i + 1) % count, i) for i in range(ends)]),
            ],
            axis=dim,
        )
    return cells


def transfer_rates(diffusivity, wind_x, wind_y, vertical_mixing):
    east_rate = diffusivity + jnp.maximum(-wind_x, 0.0)
    west_rate = diffusivity + jnp.maximum(wind_x, 0.0)
    north_rate = diffusivity + jnp.maximum(-wind_y, 0.0)
    south_rate = diffusivity + jnp.maximum(wind_y, 0.0)
    return jnp.stack(
        [east_rate, west_rate, north_rate, south_rate, vertical_mixing, vertical_mixing]
    )


def apply_transpose(padded, rates_pad, retained):
    center = padded[..., 1:-1, 1:-1, 1:-1]
    summed = retained * center
    summed = summed + rates_pad[0, 1:-1, :-2, 1:-1] * padded[..., 1:-1, :-2, 1:-1]
    summed = summed + rates_pad[1, 1:-1, 2:, 1:-1] * padded[..., 1:-1, 2:, 1:-1]
    summed = summed + rates_pad[2, 1:-1, 1:-1, :-2] * padded[..., 1:-1, 1:-1, :-2]
    summed = summed + rates_pad[3, 1:-1, 1:-1, 2:] * padded[..., 1:-1, 1:-1, 2:]
    summed = summed + rates_pad[4, :-2, 1:-1, 1:-1] * padded[..., :-2, 1:-1, 1:-1]
    summed = summed + rates_pad[5, 2:, 1:-1, 1:-1] * padded[..., 2:, 1:-1, 1:-1]
    return summed


def fourier_tables(horizon):
    freq_rows = jnp.arange(horizon, dtype=jnp.int32)
    phase_int = freq_rows[:, None] * freq_rows[None, :] % horizon
    angles = phase_int.astype(jnp.float32) * (2.0 * math.pi / horizon)
    return (jnp.cos(angles), jnp.sin(angles))


def rotation(horizon, freq_count):
    freq_rows = jnp.arange(freq_count, dtype=jnp.int32)
    angles = freq_rows.astype(jnp.float32) * (2.0 * math.pi / horizon)
    return (jnp.cos(angles)[:, None, None, None], jnp.sin(angles)[:, None, None, None])


def rotate_step(source, applied, cos_freq, sin_freq, beta_step):
    real_part = source[0] + beta_step * (cos_freq * applied[0] - sin_freq * applied[1])
    imag_part = source[1] + beta_step * (sin_freq * applied[0] + cos_freq * applied[1])
    return jnp.stack([real_part, imag_part])


def matmul_exact(table, rows):
    return jnp.dot(table, rows, precision=lax.Precision.HIGHEST)


def body(adjoint_iterate, innovations, station_cells, diffusivity, wind_x, wind_y, vertical_mixing):
    time_parts = lax.axis_size("tm")
    horizon = STEPS_DEV * time_parts
    levels_local = LEV // time_parts
    time_rank = lax.axis_index("tm")
    rate_fields = transfer_rates(diffusivity, wind_x, wind_y, vertical_mixing)
    retained = 1.0 - jnp.sum(rate_fields, axis=0)

    def scatter_step(cell_ids, values):
        return jnp.zeros((LEV, TX * NY), jnp.float32).at[:, cell_ids].add(values)

    forcing = jax.vmap(scatter_step)(station_cells, innovations).reshape(STEPS_DEV, LEV, TX, NY)
    leading = from_behind(adjoint_iterate[:1], "tm", -1)
    following = jnp.concatenate([adjoint_iterate[1:], leading], axis=0)
    extended = with_halo(jnp.concatenate([rate_fields, following], axis=0), (("space", 2),), 1)
    extended = jnp.pad(extended, ((0, 0), (1, 1), (0, 0), (1, 1)))
    rates_pad = extended[:6]
    residual = forcing - adjoint_iterate + apply_transpose(extended[6:], rates_pad, retained)
    log_beta = math.log(circ_alpha) / horizon
    beta_step = math.exp(log_beta)
    step_global = (time_rank * STEPS_DEV + jnp.arange(STEPS_DEV, dtype=jnp.int32)).astype(
        jnp.float32
    )
    scaled = residual * jnp.exp(-step_global * log_beta)[:, None, None, None]
    gathered = lax.all_to_all(scaled, "tm", split_axis=1, concat_axis=0, tiled=True)
    flat_rows = gathered.reshape(horizon, -1)
    cos_table, sin_table = fourier_tables(horizon)
    real_src = matmul_exact(cos_table, flat_rows)
    imag_src = -matmul_exact(sin_table, flat_rows)
    source = jnp.stack([real_src, imag_src]).reshape(2, horizon, levels_local, TX, NY)
    cos_freq, sin_freq = rotation(horizon, horizon)
    level_start = time_rank * levels_local
    local_rates = lax.dynamic_slice_in_dim(rates_pad, level_start, levels_local + 2, 1)
    local_retained = lax.dynamic_slice_in_dim(retained, level_start, levels_local, 0)
    iterate = source
    for sweep_index in range(INNER):
        padded = with_halo(iterate, (("tm", 2), ("space", 3)), 1)
        padded = jnp.pad(padded, ((0, 0), (0, 0), (0, 0), (0, 0), (1, 1)))
        applied = apply_transpose(padded, local_rates, local_retained)
        iterate = rotate_step(source, applied, cos_freq, sin_freq, beta_step)
    real_rows = iterate[0].reshape(horizon, -1)
    imag_rows = iterate[1].reshape(horizon, -1)
    restored = (matmul_exact(cos_table, real_rows) - matmul_exact(sin_table, imag_rows)) / horizon
    restored = restored.reshape(horizon, levels_local, TX, NY)
    returned = lax.all_to_all(restored, "tm", split_axis=0, concat_axis=1, tiled=True)
    correction = returned * jnp.exp(step_global * log_beta)[:, None, None, None]
    return adjoint_iterate + correction


def solution(mesh):
    in_specs = (
        P("tm", None, "space", None),
        P("tm", None, "space"),
        P("tm", "space"),
        P(None, "space", None),
        P(None, "space", None),
        P(None, "space", None),
        P(None, "space", None),
    )
    out_specs = P("tm", None, "space", None)
    return jax.shard_map(body, mesh=mesh, in_specs=in_specs, out_specs=out_specs, check_vma=False)
```

profile of v0, /device:TPU:0, one launch (start us, length us, event | category | flops | bytes accessed | tf_op | source)
XLA Modules:
  0.0 212.5 jit_solution(13806551617667307890)
XLA Ops:
  0.0 1.1 copy.23
  1.2 1.3 collective-permute-start
  11.1 5.0 %collective-permute-start.1 = (f32[14,16,1,128]{3,1,2,0:T(8,128)S(1)}, f32[14,16,1,128]{3,1,2,0:T(8,128)S(1)}, u32[]{:S(2)}, u32[]{:S(2)}) collective-permute-start(f32[14,16,1,128]{3,1,2,0:T(8,128)S(1)} %get-tuple-element.41), channel_id=1, source_target_pairs={{0,1},{1,2},{2,3},{4,5},{5,6},{6,7},{8,9},{9,10},{10,11},{12,13},{... | collective-permute-start | bytes 344072 | tf_op jit(solution)/shard_map/ppermute | solution.py:29
  16.1 1.3 collective-permute-start.2
  18.5 8.2 %scatter_custom_fusion = f32[8192,16]{1,0:T(8,128)} fusion(s32[1024]{0:T(1024)S(1)} %select_bitcast_fusion, f32[1024,16]{1,0:T(8,128)S(1)} %bitcast.87, f32[]{:T(128)} %constant.20.clone.1), kind=kCustom, calls=%fused_computation.35 | custom fusion | flops 16384 | bytes 524292
  26.7 2.9 %copy.48 = f32[8,1024,16]{1,0,2:T(8,128)S(1)} copy(f32[8,1024,16]{2,1,0:T(8,128)} %bitcast.71) | data formatting | bytes 1048576
  29.6 1.5 select_maximum_fusion.19
  31.3 1.6 copy-done
  33.8 14.0 %all_to_all.33 = f32[8,16,8,128]{3,2,0,1:T(8,128)S(1)} all-to-all(f32[8,16,8,128]{3,2,0,1:T(8,128)S(1)} %copy.37), channel_id=1, replica_groups=mesh['tm'=8,'space'=4] {'tm'}, dimensions={1} | all-to-all | bytes 1048576 | tf_op jit(solution)/shard_map/all_to_all | solution.py:107
  52.0 2.1 collective-permute-start.3
  54.1 1.3 collective-permute-start.4
  55.4 2.8 %collective-permute-done.4 = f32[2,64,1,8,128]{4,3,2,1,0:T(8,128)} collective-permute-done((f32[2,64,1,8,128]{4,3,2,1,0:T(8,128)}, f32[2,64,1,8,128]{4,3,2,1,0:T(8,128)}, u32[]{:S(2)}, u32[]{:S(2)}) %collective-permute-start.4) | collective-permute-done | bytes 524320 | tf_op jit(solution)/shard_map/ppermute | solution.py:31
  58.3 2.6 %pad_maximum_fusion.63 = (f32[2,64,4,1,128]{4,3,2,1,0:T(1,128)}, f32[2,64,4,1,128]{4,3,2,1,0:T(1,128)}) fusion(f32[2,64,1,8,128]{4,3,2,1,0:T(8,128)} %collective-permute-done.4, f32[2,64,2,8,128]{4,3,2,1,0:T(8,128)S(1)} %constant_dynamic-update-slice_fusion.2, f32[2,64,1,8,128]{4,3,2,1,0:T(8,128)} %collective-permute-done.3), kind=kLoop, calls=%fused_computation.205 | loop fusion | flops 262144 | bytes 2621440 | tf_op jit(solution)/shard_map/slice | solution.py:26
  60.9 4.5 %collective-permute-start.5 = (f32[2,64,4,1,128]{4,3,2,1,0:T(1,128)}, f32[2,64,4,1,128]{4,3,2,1,0:T(1,128)S(1)}, u32[]{:S(2)}, u32[]{:S(2)}) collective-permute-start(f32[2,64,4,1,128]{4,3,2,1,0:T(1,128)} %get-tuple-element.15), channel_id=1, source_target_pairs={{0,1},{1,2},{2,3},{4,5},{5,6},{6,7},{8,9},{9,10},{10,11},{12,13},{... | collective-permute-start | bytes 786440 | tf_op jit(solution)/shard_map/ppermute | solution.py:29
  65.5 1.3 collective-permute-start.6
  67.1 2.6 %collective-permute-done.5 = f32[2,64,4,1,128]{4,3,2,1,0:T(1,128)S(1)} collective-permute-done((f32[2,64,4,1,128]{4,3,2,1,0:T(1,128)}, f32[2,64,4,1,128]{4,3,2,1,0:T(1,128)S(1)}, u32[]{:S(2)}, u32[]{:S(2)}) %collective-permute-start.5) | collective-permute-done | bytes 262176 | tf_op jit(solution)/shard_map/ppermute | solution.py:29
  69.6 4.4 %collective-permute-done.6 = f32[2,64,4,1,128]{4,3,2,1,0:T(1,128)} collective-permute-done((f32[2,64,4,1,128]{4,3,2,1,0:T(1,128)}, f32[2,64,4,1,128]{4,3,2,1,0:T(1,128)}, u32[]{:S(2)}, u32[]{:S(2)}) %collective-permute-start.6) | collective-permute-done | bytes 262176 | tf_op jit(solution)/shard_map/ppermute | solution.py:31
  74.0 7.3 %select_maximum_fusion.15 = f32[2,64,4,10,130]{4,3,2,1,0:T(8,128)S(1)} fusion(f32[2,64,4,1,128]{4,3,2,1,0:T(1,128)} %collective-permute-done.6, f32[2,64,4,1,128]{4,3,2,1,0:T(1,128)S(1)} %collective-permute-done.5, f32[2,64,1,8,128]{4,3,2,1,0:T(8,128)} %collective-permute-done.4, f32[2,64,2,8,128]{4,3,2,1,0:T(8,128)S(1)} %constant_dynamic-update-slice_fusion.2, ...), kind=kLoop, calls=%fused_computation.18 | loop fusion | flops 7987200 | bytes 5283840 | tf_op jit(solution)/shard_map/concatenate | solution.py:27
  81.4 2.3 %fusion.42 = f32[2,64,2,8,128]{4,3,2,1,0:T(8,128)S(1)} fusion(f32[2,64,1,8,128]{4,3,2,1,0:T(8,128)} %collective-permute-done.4, f32[2,64,2,8,128]{4,3,2,1,0:T(8,128)S(1)} %constant_dynamic-update-slice_fusion.2, f32[2,64,1,8,128]{4,3,2,1,0:T(8,128)} %collective-permute-done.3, f32[2,64,4,10,130]{4,3,2,1,0:T(8,128)S(1)} %select_maximum_fusion.15, ...), kind=kLoop, calls=%fused_computation.130 | loop fusion | flops 5505024 | bytes 5824512 | tf_op jit(solution)/shard_map/add | solution.py:56
  84.0 10.7 %collective-permute-start.7 = (f32[2,64,1,8,128]{4,3,2,1,0:T(8,128)S(1)}, f32[2,64,1,8,128]{4,3,2,1,0:T(8,128)S(1)}, u32[]{:S(2)}, u32[]{:S(2)}) collective-permute-start(f32[2,64,1,8,128]{4,3,2,1,0:T(8,128)S(1)} %get-tuple-element.35), channel_id=1, source_target_pairs={{0,4},{4,8},{8,12},{12,16},{16,20},{20,24},{24,28},{1,5},{5,9},{9,... | collective-permute-start | bytes 1572872 | tf_op jit(solution)/shard_map/ppermute | solution.py:29
  94.7 1.5 collective-permute-start.8
  96.2 5.3 %collective-permute-done.8 = f32[2,64,1,8,128]{4,3,2,1,0:T(8,128)S(1)} collective-permute-done((f32[2,64,1,8,128]{4,3,2,1,0:T(8,128)S(1)}, f32[2,64,1,8,128]{4,3,2,1,0:T(8,128)S(1)}, u32[]{:S(2)}, u32[]{:S(2)}) %collective-permute-start.8) | collective-permute-done | bytes 524320 | tf_op jit(solution)/shard_map/ppermute | solution.py:31
  101.8 3.5 %collective-permute-start.9 = (f32[2,64,4,1,128]{4,3,2,1,0:T(1,128)S(1)}, f32[2,64,4,1,128]{4,3,2,1,0:T(1,128)S(1)}, u32[]{:S(2)}, u32[]{:S(2)}) collective-permute-start(f32[2,64,4,1,128]{4,3,2,1,0:T(1,128)S(1)} %get-tuple-element.13), channel_id=1, source_target_pairs={{0,1},{1,2},{2,3},{4,5},{5,6},{6,7},{8,9},{9,10},{10,11},{12,13},{... | collective-permute-start | bytes 786440 | tf_op jit(solution)/shard_map/ppermute | solution.py:29
  105.3 1.3 collective-permute-start.10
  106.6 2.6 %collective-permute-done.9 = f32[2,64,4,1,128]{4,3,2,1,0:T(1,128)S(1)} collective-permute-done((f32[2,64,4,1,128]{4,3,2,1,0:T(1,128)S(1)}, f32[2,64,4,1,128]{4,3,2,1,0:T(1,128)S(1)}, u32[]{:S(2)}, u32[]{:S(2)}) %collective-permute-start.9) | collective-permute-done | bytes 262176 | tf_op jit(solution)/shard_map/ppermute | solution.py:29
  109.1 4.4 %collective-permute-done.10 = f32[2,64,4,1,128]{4,3,2,1,0:T(1,128)S(1)} collective-permute-done((f32[2,64,4,1,128]{4,3,2,1,0:T(1,128)S(1)}, f32[2,64,4,1,128]{4,3,2,1,0:T(1,128)S(1)}, u32[]{:S(2)}, u32[]{:S(2)}) %collective-permute-start.10) | collective-permute-done | bytes 262176 | tf_op jit(solution)/shard_map/ppermute | solution.py:31
  113.5 6.7 %select_maximum_fusion.10 = f32[2,64,4,10,130]{4,3,2,1,0:T(8,128)S(1)} fusion(f32[2,64,4,1,128]{4,3,2,1,0:T(1,128)S(1)} %collective-permute-done.10, f32[2,64,4,1,128]{4,3,2,1,0:T(1,128)S(1)} %collective-permute-done.9, f32[2,64,1,8,128]{4,3,2,1,0:T(8,128)S(1)} %collective-permute-done.8, f32[2,64,1,8,128]{4,3,2,1,0:T(8,128)S(1)} %collective-permute-done.7, ...), kind=kLoop, calls=%fused_computation.13 | loop fusion | flops 9318400 | bytes 5283840 | tf_op jit(solution)/shard_map/concatenate | solution.py:27
  120.2 1.3 fusion.28
  121.9 9.0 %collective-permute-start.11 = (f32[2,64,1,8,128]{4,3,2,1,0:T(8,128)S(1)}, f32[2,64,1,8,128]{4,3,2,1,0:T(8,128)S(1)}, u32[]{:S(2)}, u32[]{:S(2)}) collective-permute-start(f32[2,64,1,8,128]{4,3,2,1,0:T(8,128)S(1)} %get-tuple-element.33), channel_id=1, source_target_pairs={{0,4},{4,8},{8,12},{12,16},{16,20},{20,24},{24,28},{1,5},{5,9},{9,... | collective-permute-start | bytes 1572872 | tf_op jit(solution)/shard_map/ppermute | solution.py:29
  130.9 1.3 collective-permute-start.12
  132.3 4.1 %collective-permute-done.12 = f32[2,64,1,8,128]{4,3,2,1,0:T(8,128)S(1)} collective-permute-done((f32[2,64,1,8,128]{4,3,2,1,0:T(8,128)S(1)}, f32[2,64,1,8,128]{4,3,2,1,0:T(8,128)S(1)}, u32[]{:S(2)}, u32[]{:S(2)}) %collective-permute-start.12) | collective-permute-done | bytes 524320 | tf_op jit(solution)/shard_map/ppermute | solution.py:31
  136.8 3.5 %collective-permute-start.13 = (f32[2,64,4,1,128]{4,3,2,1,0:T(1,128)S(1)}, f32[2,64,4,1,128]{4,3,2,1,0:T(1,128)S(1)}, u32[]{:S(2)}, u32[]{:S(2)}) collective-permute-start(f32[2,64,4,1,128]{4,3,2,1,0:T(1,128)S(1)} %get-tuple-element.11), channel_id=1, source_target_pairs={{0,1},{1,2},{2,3},{4,5},{5,6},{6,7},{8,9},{9,10},{10,11},{12,13},{... | collective-permute-start | bytes 786440 | tf_op jit(solution)/shard_map/ppermute | solution.py:29
  140.3 1.3 collective-permute-start.14
  141.6 2.6 %collective-permute-done.13 = f32[2,64,4,1,128]{4,3,2,1,0:T(1,128)S(1)} collective-permute-done((f32[2,64,4,1,128]{4,3,2,1,0:T(1,128)S(1)}, f32[2,64,4,1,128]{4,3,2,1,0:T(1,128)S(1)}, u32[]{:S(2)}, u32[]{:S(2)}) %collective-permute-start.13) | collective-permute-done | bytes 262176 | tf_op jit(solution)/shard_map/ppermute | solution.py:29
  144.1 4.4 %collective-permute-done.14 = f32[2,64,4,1,128]{4,3,2,1,0:T(1,128)S(1)} collective-permute-done((f32[2,64,4,1,128]{4,3,2,1,0:T(1,128)S(1)}, f32[2,64,4,1,128]{4,3,2,1,0:T(1,128)S(1)}, u32[]{:S(2)}, u32[]{:S(2)}) %collective-permute-start.14) | collective-permute-done | bytes 262176 | tf_op jit(solution)/shard_map/ppermute | solution.py:31
  148.5 6.7 %select_maximum_fusion.5 = f32[2,64,4,10,130]{4,3,2,1,0:T(8,128)S(1)} fusion(f32[2,64,4,1,128]{4,3,2,1,0:T(1,128)S(1)} %collective-permute-done.14, f32[2,64,4,1,128]{4,3,2,1,0:T(1,128)S(1)} %collective-permute-done.13, f32[2,64,1,8,128]{4,3,2,1,0:T(8,128)S(1)} %collective-permute-done.12, f32[2,64,1,8,128]{4,3,2,1,0:T(8,128)S(1)} %collective-permute-done.11, ...), kind=kLoop, calls=%fused_computation.8 | loop fusion | flops 9318400 | bytes 5283840 | tf_op jit(solution)/shard_map/concatenate | solution.py:27
  155.2 1.3 fusion.21
  156.9 8.0 %collective-permute-start.15 = (f32[2,64,1,8,128]{4,3,2,1,0:T(8,128)S(1)}, f32[2,64,1,8,128]{4,3,2,1,0:T(8,128)S(1)}, u32[]{:S(2)}, u32[]{:S(2)}) collective-permute-start(f32[2,64,1,8,128]{4,3,2,1,0:T(8,128)S(1)} %get-tuple-element.31), channel_id=1, source_target_pairs={{0,4},{4,8},{8,12},{12,16},{16,20},{20,24},{24,28},{1,5},{5,9},{9,... | collective-permute-start | bytes 1572872 | tf_op jit(solution)/shard_map/ppermute | solution.py:29
  164.9 1.3 collective-permute-start.16
  166.4 4.1 %collective-permute-done.16 = f32[2,64,1,8,128]{4,3,2,1,0:T(8,128)S(1)} collective-permute-done((f32[2,64,1,8,128]{4,3,2,1,0:T(8,128)S(1)}, f32[2,64,1,8,128]{4,3,2,1,0:T(8,128)S(1)}, u32[]{:S(2)}, u32[]{:S(2)}) %collective-permute-start.16) | collective-permute-done | bytes 524320 | tf_op jit(solution)/shard_map/ppermute | solution.py:31
  170.7 2.5 %collective-permute-start.17 = (f32[2,64,4,1,128]{4,3,2,1,0:T(1,128)S(1)}, f32[2,64,4,1,128]{4,3,2,1,0:T(1,128)S(1)}, u32[]{:S(2)}, u32[]{:S(2)}) collective-permute-start(f32[2,64,4,1,128]{4,3,2,1,0:T(1,128)S(1)} %get-tuple-element.9), channel_id=1, source_target_pairs={{0,1},{1,2},{2,3},{4,5},{5,6},{6,7},{8,9},{9,10},{10,11},{12,13},{... | collective-permute-start | bytes 786440 | tf_op jit(solution)/shard_map/ppermute | solution.py:29
  173.2 1.4 collective-permute-start.18
  174.7 2.4 %collective-permute-done.17 = f32[2,64,4,1,128]{4,3,2,1,0:T(1,128)S(1)} collective-permute-done((f32[2,64,4,1,128]{4,3,2,1,0:T(1,128)S(1)}, f32[2,64,4,1,128]{4,3,2,1,0:T(1,128)S(1)}, u32[]{:S(2)}, u32[]{:S(2)}) %collective-permute-start.17) | collective-permute-done | bytes 262176 | tf_op jit(solution)/shard_map/ppermute | solution.py:29
  177.1 4.6 %collective-permute-done.18 = f32[2,64,4,1,128]{4,3,2,1,0:T(1,128)S(1)} collective-permute-done((f32[2,64,4,1,128]{4,3,2,1,0:T(1,128)S(1)}, f32[2,64,4,1,128]{4,3,2,1,0:T(1,128)S(1)}, u32[]{:S(2)}, u32[]{:S(2)}) %collective-permute-start.18) | collective-permute-done | bytes 262176 | tf_op jit(solution)/shard_map/ppermute | solution.py:31
  181.6 6.7 %select_maximum_fusion = f32[2,64,4,10,130]{4,3,2,1,0:T(8,128)S(1)} fusion(f32[2,64,4,1,128]{4,3,2,1,0:T(1,128)S(1)} %collective-permute-done.18, f32[2,64,4,1,128]{4,3,2,1,0:T(1,128)S(1)} %collective-permute-done.17, f32[2,64,1,8,128]{4,3,2,1,0:T(8,128)S(1)} %collective-permute-done.16, f32[2,64,1,8,128]{4,3,2,1,0:T(8,128)S(1)} %collective-permute-done.15, ...), kind=kLoop, calls=%fused_computation.3 | loop fusion | flops 9318400 | bytes 5283840 | tf_op jit(solution)/shard_map/concatenate | solution.py:27
  188.3 1.3 fusion.14
  192.3 9.5 %all-to-all-start.1 = ((f32[64,2,8,128]{3,2,1,0:T(8,128)}), f32[64,2,8,128]{3,2,1,0:T(8,128)S(1)}, u32[]{:S(2)}, u32[]{:S(2)}) async-start(f32[64,2,8,128]{3,2,1,0:T(8,128)} %bitcast.42), calls=%async_computation.1 | async-start | bytes 1048576 | tf_op jit(solution)/shard_map/all_to_all | solution.py:127
  201.8 9.7 %all-to-all-done.1 = f32[64,2,8,128]{3,2,1,0:T(8,128)S(1)} async-done(((f32[64,2,8,128]{3,2,1,0:T(8,128)}), f32[64,2,8,128]{3,2,1,0:T(8,128)S(1)}, u32[]{:S(2)}, u32[]{:S(2)}) %all-to-all-start.1) | async-done | bytes 524320 | tf_op jit(solution)/shard_map/all_to_all | solution.py:127
  (84 shorter events, 21.2 us)
Async XLA Ops:
  1.2 10.0 %collective-permute-start = (f32[1,16,8,128]{3,1,2,0:T(8,128)S(1)}, f32[1,16,8,128]{3,1,2,0:T(8,128)S(1)}, u32[]{:S(2)}, u32[]{:S(2)}) collective-permute-start(f32[1,16,8,128]{3,1,2,0:T(8,128)S(1)} %slice.399), channel_id=1, source_target_pairs={{4,0},{8,4},{12,8},{16,12},{20,16},{24,20},{28,24},{5,1},{9,5},{13... | collective-permute-start | bytes 196616 | tf_op jit(solution)/shard_map/ppermute | solution.py:18
  9.6 23.3 %copy-start.3 = (f32[8,16,8,128]{3,2,1,0:T(8,128)S(1)}, f32[8,16,8,128]{3,2,1,0:T(8,128)}, u32[]{:S(2)}) copy-start(f32[8,16,8,128]{3,2,1,0:T(8,128)} %param.7) | copy-start | bytes 1572868
  11.1 18.5 %collective-permute-start.1 = (f32[14,16,1,128]{3,1,2,0:T(8,128)S(1)}, f32[14,16,1,128]{3,1,2,0:T(8,128)S(1)}, u32[]{:S(2)}, u32[]{:S(2)}) collective-permute-start(f32[14,16,1,128]{3,1,2,0:T(8,128)S(1)} %get-tuple-element.41), channel_id=1, source_target_pairs={{0,1},{1,2},{2,3},{4,5},{5,6},{6,7},{8,9},{9,10},{10,11},{12,13},{... | collective-permute-start | bytes 344072 | tf_op jit(solution)/shard_map/ppermute | solution.py:29
  16.1 13.5 %collective-permute-start.2 = (f32[14,16,1,128]{3,1,2,0:T(8,128)S(1)}, f32[14,16,1,128]{3,1,2,0:T(8,128)S(1)}, u32[]{:S(2)}, u32[]{:S(2)}) collective-permute-start(f32[14,16,1,128]{3,1,2,0:T(8,128)S(1)} %get-tuple-element.42), channel_id=1, source_target_pairs={{1,0},{2,1},{3,2},{5,4},{6,5},{7,6},{9,8},{10,9},{11,10},{13,12},{... | collective-permute-start | bytes 344072 | tf_op jit(solution)/shard_map/ppermute | solution.py:31
  31.1 1.7 copy-start
  33.7 33.1 %slice-start = ((f32[14,18,10,130]{3,1,2,0:T(8,128)}), f32[6,18,10,130]{3,1,2,0:T(8,128)S(1)}, s32[]{:S(2)}) async-start(f32[14,18,10,130]{3,1,2,0:T(8,128)} %copy-done), calls=%async_computation.2 | async-start | bytes 2949120 | tf_op jit(solution)/shard_map/slice | solution.py:99
  48.6 0.9 copy-start.5
  49.4 0.8 copy-start.7
  50.1 0.8 copy-start.1
  52.0 3.4 %collective-permute-start.3 = (f32[2,64,1,8,128]{4,3,2,1,0:T(8,128)}, f32[2,64,1,8,128]{4,3,2,1,0:T(8,128)}, u32[]{:S(2)}, u32[]{:S(2)}) collective-permute-start(f32[2,64,1,8,128]{4,3,2,1,0:T(8,128)} %get-tuple-element.37), channel_id=1, source_target_pairs={{0,4},{4,8},{8,12},{12,16},{16,20},{20,24},{24,28},{1,5},{5,9},{9,... | collective-permute-start | bytes 1572872 | tf_op jit(solution)/shard_map/ppermute | solution.py:29
  54.1 4.1 %collective-permute-start.4 = (f32[2,64,1,8,128]{4,3,2,1,0:T(8,128)}, f32[2,64,1,8,128]{4,3,2,1,0:T(8,128)}, u32[]{:S(2)}, u32[]{:S(2)}) collective-permute-start(f32[2,64,1,8,128]{4,3,2,1,0:T(8,128)} %get-tuple-element.38), channel_id=1, source_target_pairs={{4,0},{8,4},{12,8},{16,12},{20,16},{24,20},{28,24},{5,1},{9,5},{13... | collective-permute-start | bytes 1572872 | tf_op jit(solution)/shard_map/ppermute | solution.py:31
  60.9 8.7 %collective-permute-start.5 = (f32[2,64,4,1,128]{4,3,2,1,0:T(1,128)}, f32[2,64,4,1,128]{4,3,2,1,0:T(1,128)S(1)}, u32[]{:S(2)}, u32[]{:S(2)}) collective-permute-start(f32[2,64,4,1,128]{4,3,2,1,0:T(1,128)} %get-tuple-element.15), channel_id=1, source_target_pairs={{0,1},{1,2},{2,3},{4,5},{5,6},{6,7},{8,9},{9,10},{10,11},{12,13},{... | collective-permute-start | bytes 786440 | tf_op jit(solution)/shard_map/ppermute | solution.py:29
  65.5 8.6 %collective-permute-start.6 = (f32[2,64,4,1,128]{4,3,2,1,0:T(1,128)}, f32[2,64,4,1,128]{4,3,2,1,0:T(1,128)}, u32[]{:S(2)}, u32[]{:S(2)}) collective-permute-start(f32[2,64,4,1,128]{4,3,2,1,0:T(1,128)} %get-tuple-element.16), channel_id=1, source_target_pairs={{1,0},{2,1},{3,2},{5,4},{6,5},{7,6},{9,8},{10,9},{11,10},{13,12},{... | collective-permute-start | bytes 786440 | tf_op jit(solution)/shard_map/ppermute | solution.py:31
  67.1 16.6 %copy-start.2 = (f32[8,8,16,128]{3,2,1,0:T(8,128)S(1)}, f32[8,8,16,128]{3,2,1,0:T(8,128)}, u32[]{:S(2)}) copy-start(f32[8,8,16,128]{3,2,1,0:T(8,128)} %copy-done.1) | copy-start | bytes 1572868
  84.0 12.2 %collective-permute-start.7 = (f32[2,64,1,8,128]{4,3,2,1,0:T(8,128)S(1)}, f32[2,64,1,8,128]{4,3,2,1,0:T(8,128)S(1)}, u32[]{:S(2)}, u32[]{:S(2)}) collective-permute-start(f32[2,64,1,8,128]{4,3,2,1,0:T(8,128)S(1)} %get-tuple-element.35), channel_id=1, source_target_pairs={{0,4},{4,8},{8,12},{12,16},{16,20},{20,24},{24,28},{1,5},{5,9},{9,... | collective-permute-start | bytes 1572872 | tf_op jit(solution)/shard_map/ppermute | solution.py:29
  94.7 6.8 %collective-permute-start.8 = (f32[2,64,1,8,128]{4,3,2,1,0:T(8,128)S(1)}, f32[2,64,1,8,128]{4,3,2,1,0:T(8,128)S(1)}, u32[]{:S(2)}, u32[]{:S(2)}) collective-permute-start(f32[2,64,1,8,128]{4,3,2,1,0:T(8,128)S(1)} %get-tuple-element.36), channel_id=1, source_target_pairs={{4,0},{8,4},{12,8},{16,12},{20,16},{24,20},{28,24},{5,1},{9,5},{13... | collective-permute-start | bytes 1572872 | tf_op jit(solution)/shard_map/ppermute | solution.py:31
  101.8 7.3 %collective-permute-start.9 = (f32[2,64,4,1,128]{4,3,2,1,0:T(1,128)S(1)}, f32[2,64,4,1,128]{4,3,2,1,0:T(1,128)S(1)}, u32[]{:S(2)}, u32[]{:S(2)}) collective-permute-start(f32[2,64,4,1,128]{4,3,2,1,0:T(1,128)S(1)} %get-tuple-element.13), channel_id=1, source_target_pairs={{0,1},{1,2},{2,3},{4,5},{5,6},{6,7},{8,9},{9,10},{10,11},{12,13},{... | collective-permute-start | bytes 786440 | tf_op jit(solution)/shard_map/ppermute | solution.py:29
  105.3 8.3 %collective-permute-start.10 = (f32[2,64,4,1,128]{4,3,2,1,0:T(1,128)S(1)}, f32[2,64,4,1,128]{4,3,2,1,0:T(1,128)S(1)}, u32[]{:S(2)}, u32[]{:S(2)}) collective-permute-start(f32[2,64,4,1,128]{4,3,2,1,0:T(1,128)S(1)} %get-tuple-element.14), channel_id=1, source_target_pairs={{1,0},{2,1},{3,2},{5,4},{6,5},{7,6},{9,8},{10,9},{11,10},{13,12},{... | collective-permute-start | bytes 786440 | tf_op jit(solution)/shard_map/ppermute | solution.py:31
  121.9 10.5 %collective-permute-start.11 = (f32[2,64,1,8,128]{4,3,2,1,0:T(8,128)S(1)}, f32[2,64,1,8,128]{4,3,2,1,0:T(8,128)S(1)}, u32[]{:S(2)}, u32[]{:S(2)}) collective-permute-start(f32[2,64,1,8,128]{4,3,2,1,0:T(8,128)S(1)} %get-tuple-element.33), channel_id=1, source_target_pairs={{0,4},{4,8},{8,12},{12,16},{16,20},{20,24},{24,28},{1,5},{5,9},{9,... | collective-permute-start | bytes 1572872 | tf_op jit(solution)/shard_map/ppermute | solution.py:29
  130.9 5.6 %collective-permute-start.12 = (f32[2,64,1,8,128]{4,3,2,1,0:T(8,128)S(1)}, f32[2,64,1,8,128]{4,3,2,1,0:T(8,128)S(1)}, u32[]{:S(2)}, u32[]{:S(2)}) collective-permute-start(f32[2,64,1,8,128]{4,3,2,1,0:T(8,128)S(1)} %get-tuple-element.34), channel_id=1, source_target_pairs={{4,0},{8,4},{12,8},{16,12},{20,16},{24,20},{28,24},{5,1},{9,5},{13... | collective-permute-start | bytes 1572872 | tf_op jit(solution)/shard_map/ppermute | solution.py:31
  136.8 7.3 %collective-permute-start.13 = (f32[2,64,4,1,128]{4,3,2,1,0:T(1,128)S(1)}, f32[2,64,4,1,128]{4,3,2,1,0:T(1,128)S(1)}, u32[]{:S(2)}, u32[]{:S(2)}) collective-permute-start(f32[2,64,4,1,128]{4,3,2,1,0:T(1,128)S(1)} %get-tuple-element.11), channel_id=1, source_target_pairs={{0,1},{1,2},{2,3},{4,5},{5,6},{6,7},{8,9},{9,10},{10,11},{12,13},{... | collective-permute-start | bytes 786440 | tf_op jit(solution)/shard_map/ppermute | solution.py:29
  140.3 8.3 %collective-permute-start.14 = (f32[2,64,4,1,128]{4,3,2,1,0:T(1,128)S(1)}, f32[2,64,4,1,128]{4,3,2,1,0:T(1,128)S(1)}, u32[]{:S(2)}, u32[]{:S(2)}) collective-permute-start(f32[2,64,4,1,128]{4,3,2,1,0:T(1,128)S(1)} %get-tuple-element.12), channel_id=1, source_target_pairs={{1,0},{2,1},{3,2},{5,4},{6,5},{7,6},{9,8},{10,9},{11,10},{13,12},{... | collective-permute-start | bytes 786440 | tf_op jit(solution)/shard_map/ppermute | solution.py:31
  156.9 9.5 %collective-permute-start.15 = (f32[2,64,1,8,128]{4,3,2,1,0:T(8,128)S(1)}, f32[2,64,1,8,128]{4,3,2,1,0:T(8,128)S(1)}, u32[]{:S(2)}, u32[]{:S(2)}) collective-permute-start(f32[2,64,1,8,128]{4,3,2,1,0:T(8,128)S(1)} %get-tuple-element.31), channel_id=1, source_target_pairs={{0,4},{4,8},{8,12},{12,16},{16,20},{20,24},{24,28},{1,5},{5,9},{9,... | collective-permute-start | bytes 1572872 | tf_op jit(solution)/shard_map/ppermute | solution.py:29
  164.9 5.5 %collective-permute-start.16 = (f32[2,64,1,8,128]{4,3,2,1,0:T(8,128)S(1)}, f32[2,64,1,8,128]{4,3,2,1,0:T(8,128)S(1)}, u32[]{:S(2)}, u32[]{:S(2)}) collective-permute-start(f32[2,64,1,8,128]{4,3,2,1,0:T(8,128)S(1)} %get-tuple-element.32), channel_id=1, source_target_pairs={{4,0},{8,4},{12,8},{16,12},{20,16},{24,20},{28,24},{5,1},{9,5},{13... | collective-permute-start | bytes 1572872 | tf_op jit(solution)/shard_map/ppermute | solution.py:31
  170.7 6.3 %collective-permute-start.17 = (f32[2,64,4,1,128]{4,3,2,1,0:T(1,128)S(1)}, f32[2,64,4,1,128]{4,3,2,1,0:T(1,128)S(1)}, u32[]{:S(2)}, u32[]{:S(2)}) collective-permute-start(f32[2,64,4,1,128]{4,3,2,1,0:T(1,128)S(1)} %get-tuple-element.9), channel_id=1, source_target_pairs={{0,1},{1,2},{2,3},{4,5},{5,6},{6,7},{8,9},{9,10},{10,11},{12,13},{... | collective-permute-start | bytes 786440 | tf_op jit(solution)/shard_map/ppermute | solution.py:29
  173.2 16.6 %copy-start.8 = (f32[64,2048]{1,0:T(8,128)S(1)}, f32[64,2048]{1,0:T(8,128)}, u32[]{:S(2)}) copy-start(f32[64,2048]{1,0:T(8,128)} %copy-done.7) | copy-start | bytes 1572868
  173.2 8.4 %collective-permute-start.18 = (f32[2,64,4,1,128]{4,3,2,1,0:T(1,128)S(1)}, f32[2,64,4,1,128]{4,3,2,1,0:T(1,128)S(1)}, u32[]{:S(2)}, u32[]{:S(2)}) collective-permute-start(f32[2,64,4,1,128]{4,3,2,1,0:T(1,128)S(1)} %get-tuple-element.10), channel_id=1, source_target_pairs={{1,0},{2,1},{3,2},{5,4},{6,5},{7,6},{9,8},{10,9},{11,10},{13,12},{... | collective-permute-start | bytes 786440 | tf_op jit(solution)/shard_map/ppermute | solution.py:31
  188.3 2.3 %copy-start.6 = (f32[64,2048]{1,0:T(8,128)S(1)}, f32[64,2048]{1,0:T(8,128)}, u32[]{:S(2)}) copy-start(f32[64,2048]{1,0:T(8,128)} %copy-done.5) | copy-start | bytes 1572868
  188.3 23.2 %copy-start.4 = (f32[8,16,8,128]{3,2,1,0:T(8,128)S(1)}, f32[8,16,8,128]{3,2,1,0:T(8,128)}, u32[]{:S(2)}) copy-start(f32[8,16,8,128]{3,2,1,0:T(8,128)} %param.7) | copy-start | bytes 1572868
  192.3 19.2 %all-to-all-start.1 = ((f32[64,2,8,128]{3,2,1,0:T(8,128)}), f32[64,2,8,128]{3,2,1,0:T(8,128)S(1)}, u32[]{:S(2)}, u32[]{:S(2)}) async-start(f32[64,2,8,128]{3,2,1,0:T(8,128)} %bitcast.42), calls=%async_computation.1 | async-start | bytes 1048576 | tf_op jit(solution)/shard_map/all_to_all | solution.py:127
where the time goes:
time: 214 us; the launch traced here: 212 us
  starting transfers between devices  71.4 us (33%)
  other arithmetic  56.4 us (26%)
  waiting for transfers between devices  54.2 us (25%)
  blocking collectives  14 us (7%)
  local copies, waits for them, and re-layouts  12.8 us (6%)
  matrix products  2.97 us (1%)
    ppermute x9, starting transfers between devices, with_halo(): lax.ppermute(tail, axis, [(i, (i + 1) % count) for i in range(ends)])  48.7 us
    ppermute x9, waiting for transfers between devices, with_halo(): lax.ppermute(head, axis, [((i + 1) % count, i) for i in range(ends)])  34.1 us
    concatenate x5, other arithmetic, with_halo(): jnp.concatenate([lax.ppermute(tail, axis, [(i, (i + 1) % count) for i in...  28.8 us
    all_to_all x1, blocking collectives, body(): lax.all_to_all(scaled, 'tm', split_axis=1, concat_axis=0, tiled=True)  14 us
    unnamed x8, other arithmetic  13.4 us
    ppermute x9, starting transfers between devices, with_halo(): lax.ppermute(head, axis, [((i + 1) % count, i) for i in range(ends)])  11.9 us
    unnamed x28, local copies, waits for them, and re-layouts  10.8 us
    ppermute x9, waiting for transfers between devices, with_halo(): lax.ppermute(tail, axis, [(i, (i + 1) % count) for i in range(ends)])  10.5 us
  transfers between devices with their start and end apart: 20, of which 15 were waited for; matrix products, arithmetic and copies ran while one was open for 10% of the time, Pallas kernels for 0%

commit v1 on v0

--- a/solution.py
+++ b/solution.py
@@ -104,7 +104,10 @@
         jnp.float32
     )
     scaled = residual * jnp.exp(-step_global * log_beta)[:, None, None, None]
-    gathered = lax.all_to_all(scaled, "tm", split_axis=1, concat_axis=0, tiled=True)
+    gathered = jnp.concatenate(
+        lax.all_to_all(jnp.stack(jnp.split(scaled, lax.axis_size("tm"), axis=1)), "tm", 0, 0),
+        axis=0,
+    )
     flat_rows = gathered.reshape(horizon, -1)
     cos_table, sin_table = fourier_tables(horizon)
     real_src = matmul_exact(cos_table, flat_rows)

time: 214 us -> 214 us (level)
    unnamed x28 -> x35, local copies, waits for them, and re-layouts: 10.8 us -> 11.1 us
where the time goes in v1:
time: 214 us; the launch traced here: 213 us
  starting transfers between devices  71.4 us (33%)
  other arithmetic  56.4 us (26%)
  waiting for transfers between devices  54.2 us (25%)
  blocking collectives  14 us (7%)
  local copies, waits for them, and re-layouts  12.9 us (6%)
  matrix products  2.96 us (1%)
    ppermute x9, starting transfers between devices, with_halo(): lax.ppermute(tail, axis, [(i, (i + 1) % count) for i in range(ends)])  48.8 us
    ppermute x9, waiting for transfers between devices, with_halo(): lax.ppermute(head, axis, [((i + 1) % count, i) for i in range(ends)])  34 us
    concatenate x5, other arithmetic, with_halo(): jnp.concatenate([lax.ppermute(tail, axis, [(i, (i + 1) % count) for i in...  28.8 us
    all_to_all x1, blocking collectives, body(): lax.all_to_all(jnp.stack(jnp.split(scaled, lax.axis_size('tm'), axis=1)),...  14 us
    unnamed x8, other arithmetic  13.4 us
    ppermute x9, starting transfers between devices, with_halo(): lax.ppermute(head, axis, [((i + 1) % count, i) for i in range(ends)])  11.9 us
    unnamed x35, local copies, waits for them, and re-layouts  11.1 us
    ppermute x9, waiting for transfers between devices, with_halo(): lax.ppermute(tail, axis, [(i, (i + 1) % count) for i in range(ends)])  10.5 us
  transfers between devices with their start and end apart: 20, of which 15 were waited for; matrix products, arithmetic and copies ran while one was open for 10% of the time, Pallas kernels for 0%

profile of v1, /device:TPU:0, one launch (start us, length us, event | category | flops | bytes accessed | tf_op | source)
XLA Modules:
  0.0 212.6 jit_solution(14876054607061578206)
XLA Ops:
  0.0 1.1 copy.47
  1.2 1.3 collective-permute-start
  11.1 5.0 %collective-permute-start.1 = (f32[14,16,1,128]{3,1,2,0:T(8,128)S(1)}, f32[14,16,1,128]{3,1,2,0:T(8,128)S(1)}, u32[]{:S(2)}, u32[]{:S(2)}) collective-permute-start(f32[14,16,1,128]{3,1,2,0:T(8,128)S(1)} %get-tuple-element.41), channel_id=1, source_target_pairs={{0,1},{1,2},{2,3},{4,5},{5,6},{6,7},{8,9},{9,10},{10,11},{12,13},{... | collective-permute-start | bytes 344072 | tf_op jit(solution)/shard_map/ppermute | solution.py:29
  16.1 1.3 collective-permute-start.2
  18.5 8.2 %scatter_custom_fusion = f32[8192,16]{1,0:T(8,128)} fusion(s32[1024]{0:T(1024)S(1)} %select_bitcast_fusion, f32[1024,16]{1,0:T(8,128)S(1)} %bitcast.113, f32[]{:T(128)} %constant.20.clone.1), kind=kCustom, calls=%fused_computation.35 | custom fusion | flops 16384 | bytes 524292
  26.7 2.9 %copy.71 = f32[8,1024,16]{1,0,2:T(8,128)S(1)} copy(f32[8,1024,16]{2,1,0:T(8,128)} %bitcast.99) | data formatting | bytes 1048576
  29.6 1.5 select_maximum_fusion.19
  31.3 1.6 copy-done
  33.9 14.0 %all_to_all.23 = f32[8,8,2,8,128]{4,2,3,1,0:T(2,128)S(1)} all-to-all(f32[8,8,2,8,128]{4,2,3,1,0:T(2,128)S(1)} %fusion.85), channel_id=1, replica_groups=mesh['tm'=8,'space'=4] {'tm'}, dimensions={0} | all-to-all | bytes 1048576 | tf_op jit(solution)/shard_map/all_to_all | solution.py:108
  52.2 2.1 collective-permute-start.3
  54.3 1.3 collective-permute-start.4
  55.6 2.8 %collective-permute-done.4 = f32[2,64,1,8,128]{4,3,2,1,0:T(8,128)} collective-permute-done((f32[2,64,1,8,128]{4,3,2,1,0:T(8,128)}, f32[2,64,1,8,128]{4,3,2,1,0:T(8,128)}, u32[]{:S(2)}, u32[]{:S(2)}) %collective-permute-start.4) | collective-permute-done | bytes 524320 | tf_op jit(solution)/shard_map/ppermute | solution.py:31
  58.4 2.6 %pad_maximum_fusion.63 = (f32[2,64,4,1,128]{4,3,2,1,0:T(1,128)}, f32[2,64,4,1,128]{4,3,2,1,0:T(1,128)}) fusion(f32[2,64,1,8,128]{4,3,2,1,0:T(8,128)} %collective-permute-done.4, f32[2,64,2,8,128]{4,3,2,1,0:T(8,128)S(1)} %constant_dynamic-update-slice_fusion.2, f32[2,64,1,8,128]{4,3,2,1,0:T(8,128)} %collective-permute-done.3), kind=kLoop, calls=%fused_computation.204 | loop fusion | flops 262144 | bytes 2621440 | tf_op jit(solution)/shard_map/slice | solution.py:26
  61.0 4.6 %collective-permute-start.5 = (f32[2,64,4,1,128]{4,3,2,1,0:T(1,128)}, f32[2,64,4,1,128]{4,3,2,1,0:T(1,128)S(1)}, u32[]{:S(2)}, u32[]{:S(2)}) collective-permute-start(f32[2,64,4,1,128]{4,3,2,1,0:T(1,128)} %get-tuple-element.15), channel_id=1, source_target_pairs={{0,1},{1,2},{2,3},{4,5},{5,6},{6,7},{8,9},{9,10},{10,11},{12,13},{... | collective-permute-start | bytes 786440 | tf_op jit(solution)/shard_map/ppermute | solution.py:29
  65.6 1.3 collective-permute-start.6
  67.2 2.6 %collective-permute-done.5 = f32[2,64,4,1,128]{4,3,2,1,0:T(1,128)S(1)} collective-permute-done((f32[2,64,4,1,128]{4,3,2,1,0:T(1,128)}, f32[2,64,4,1,128]{4,3,2,1,0:T(1,128)S(1)}, u32[]{:S(2)}, u32[]{:S(2)}) %collective-permute-start.5) | collective-permute-done | bytes 262176 | tf_op jit(solution)/shard_map/ppermute | solution.py:29
  69.8 4.4 %collective-permute-done.6 = f32[2,64,4,1,128]{4,3,2,1,0:T(1,128)} collective-permute-done((f32[2,64,4,1,128]{4,3,2,1,0:T(1,128)}, f32[2,64,4,1,128]{4,3,2,1,0:T(1,128)}, u32[]{:S(2)}, u32[]{:S(2)}) %collective-permute-start.6) | collective-permute-done | bytes 262176 | tf_op jit(solution)/shard_map/ppermute | solution.py:31
  74.2 7.3 %select_maximum_fusion.15 = f32[2,64,4,10,130]{4,3,2,1,0:T(8,128)S(1)} fusion(f32[2,64,4,1,128]{4,3,2,1,0:T(1,128)} %collective-permute-done.6, f32[2,64,4,1,128]{4,3,2,1,0:T(1,128)S(1)} %collective-permute-done.5, f32[2,64,1,8,128]{4,3,2,1,0:T(8,128)} %collective-permute-done.4, f32[2,64,2,8,128]{4,3,2,1,0:T(8,128)S(1)} %constant_dynamic-update-slice_fusion.2, ...), kind=kLoop, calls=%fused_computation.18 | loop fusion | flops 7987200 | bytes 5283840 | tf_op jit(solution)/shard_map/concatenate | solution.py:27
  81.5 2.3 %fusion.42 = f32[2,64,2,8,128]{4,3,2,1,0:T(8,128)S(1)} fusion(f32[2,64,1,8,128]{4,3,2,1,0:T(8,128)} %collective-permute-done.4, f32[2,64,2,8,128]{4,3,2,1,0:T(8,128)S(1)} %constant_dynamic-update-slice_fusion.2, f32[2,64,1,8,128]{4,3,2,1,0:T(8,128)} %collective-permute-done.3, f32[2,64,4,10,130]{4,3,2,1,0:T(8,128)S(1)} %select_maximum_fusion.15, ...), kind=kLoop, calls=%fused_computation.130 | loop fusion | flops 5505024 | bytes 5824512 | tf_op jit(solution)/shard_map/add | solution.py:56
  84.1 10.7 %collective-permute-start.7 = (f32[2,64,1,8,128]{4,3,2,1,0:T(8,128)S(1)}, f32[2,64,1,8,128]{4,3,2,1,0:T(8,128)S(1)}, u32[]{:S(2)}, u32[]{:S(2)}) collective-permute-start(f32[2,64,1,8,128]{4,3,2,1,0:T(8,128)S(1)} %get-tuple-element.35), channel_id=1, source_target_pairs={{0,4},{4,8},{8,12},{12,16},{16,20},{20,24},{24,28},{1,5},{5,9},{9,... | collective-permute-start | bytes 1572872 | tf_op jit(solution)/shard_map/ppermute | solution.py:29
  94.8 1.5 collective-permute-start.8
  96.3 5.3 %collective-permute-done.8 = f32[2,64,1,8,128]{4,3,2,1,0:T(8,128)S(1)} collective-permute-done((f32[2,64,1,8,128]{4,3,2,1,0:T(8,128)S(1)}, f32[2,64,1,8,128]{4,3,2,1,0:T(8,128)S(1)}, u32[]{:S(2)}, u32[]{:S(2)}) %collective-permute-start.8) | collective-permute-done | bytes 524320 | tf_op jit(solution)/shard_map/ppermute | solution.py:31
  101.9 3.5 %collective-permute-start.9 = (f32[2,64,4,1,128]{4,3,2,1,0:T(1,128)S(1)}, f32[2,64,4,1,128]{4,3,2,1,0:T(1,128)S(1)}, u32[]{:S(2)}, u32[]{:S(2)}) collective-permute-start(f32[2,64,4,1,128]{4,3,2,1,0:T(1,128)S(1)} %get-tuple-element.13), channel_id=1, source_target_pairs={{0,1},{1,2},{2,3},{4,5},{5,6},{6,7},{8,9},{9,10},{10,11},{12,13},{... | collective-permute-start | bytes 786440 | tf_op jit(solution)/shard_map/ppermute | solution.py:29
  105.4 1.3 collective-permute-start.10
  106.7 2.6 %collective-permute-done.9 = f32[2,64,4,1,128]{4,3,2,1,0:T(1,128)S(1)} collective-permute-done((f32[2,64,4,1,128]{4,3,2,1,0:T(1,128)S(1)}, f32[2,64,4,1,128]{4,3,2,1,0:T(1,128)S(1)}, u32[]{:S(2)}, u32[]{:S(2)}) %collective-permute-start.9) | collective-permute-done | bytes 262176 | tf_op jit(solution)/shard_map/ppermute | solution.py:29
  109.3 4.4 %collective-permute-done.10 = f32[2,64,4,1,128]{4,3,2,1,0:T(1,128)S(1)} collective-permute-done((f32[2,64,4,1,128]{4,3,2,1,0:T(1,128)S(1)}, f32[2,64,4,1,128]{4,3,2,1,0:T(1,128)S(1)}, u32[]{:S(2)}, u32[]{:S(2)}) %collective-permute-start.10) | collective-permute-done | bytes 262176 | tf_op jit(solution)/shard_map/ppermute | solution.py:31
  113.7 6.7 %select_maximum_fusion.10 = f32[2,64,4,10,130]{4,3,2,1,0:T(8,128)S(1)} fusion(f32[2,64,4,1,128]{4,3,2,1,0:T(1,128)S(1)} %collective-permute-done.10, f32[2,64,4,1,128]{4,3,2,1,0:T(1,128)S(1)} %collective-permute-done.9, f32[2,64,1,8,128]{4,3,2,1,0:T(8,128)S(1)} %collective-permute-done.8, f32[2,64,1,8,128]{4,3,2,1,0:T(8,128)S(1)} %collective-permute-done.7, ...), kind=kLoop, calls=%fused_computation.13 | loop fusion | flops 9318400 | bytes 5283840 | tf_op jit(solution)/shard_map/concatenate | solution.py:27
  120.4 1.3 fusion.28
  122.0 9.0 %collective-permute-start.11 = (f32[2,64,1,8,128]{4,3,2,1,0:T(8,128)S(1)}, f32[2,64,1,8,128]{4,3,2,1,0:T(8,128)S(1)}, u32[]{:S(2)}, u32[]{:S(2)}) collective-permute-start(f32[2,64,1,8,128]{4,3,2,1,0:T(8,128)S(1)} %get-tuple-element.33), channel_id=1, source_target_pairs={{0,4},{4,8},{8,12},{12,16},{16,20},{20,24},{24,28},{1,5},{5,9},{9,... | collective-permute-start | bytes 1572872 | tf_op jit(solution)/shard_map/ppermute | solution.py:29
  131.0 1.3 collective-permute-start.12
  132.5 4.1 %collective-permute-done.12 = f32[2,64,1,8,128]{4,3,2,1,0:T(8,128)S(1)} collective-permute-done((f32[2,64,1,8,128]{4,3,2,1,0:T(8,128)S(1)}, f32[2,64,1,8,128]{4,3,2,1,0:T(8,128)S(1)}, u32[]{:S(2)}, u32[]{:S(2)}) %collective-permute-start.12) | collective-permute-done | bytes 524320 | tf_op jit(solution)/shard_map/ppermute | solution.py:31
  136.9 3.5 %collective-permute-start.13 = (f32[2,64,4,1,128]{4,3,2,1,0:T(1,128)S(1)}, f32[2,64,4,1,128]{4,3,2,1,0:T(1,128)S(1)}, u32[]{:S(2)}, u32[]{:S(2)}) collective-permute-start(f32[2,64,4,1,128]{4,3,2,1,0:T(1,128)S(1)} %get-tuple-element.11), channel_id=1, source_target_pairs={{0,1},{1,2},{2,3},{4,5},{5,6},{6,7},{8,9},{9,10},{10,11},{12,13},{... | collective-permute-start | bytes 786440 | tf_op jit(solution)/shard_map/ppermute | solution.py:29
  140.4 1.3 collective-permute-start.14
  141.7 2.6 %collective-permute-done.13 = f32[2,64,4,1,128]{4,3,2,1,0:T(1,128)S(1)} collective-permute-done((f32[2,64,4,1,128]{4,3,2,1,0:T(1,128)S(1)}, f32[2,64,4,1,128]{4,3,2,1,0:T(1,128)S(1)}, u32[]{:S(2)}, u32[]{:S(2)}) %collective-permute-start.13) | collective-permute-done | bytes 262176 | tf_op jit(solution)/shard_map/ppermute | solution.py:29
  144.3 4.4 %collective-permute-done.14 = f32[2,64,4,1,128]{4,3,2,1,0:T(1,128)S(1)} collective-permute-done((f32[2,64,4,1,128]{4,3,2,1,0:T(1,128)S(1)}, f32[2,64,4,1,128]{4,3,2,1,0:T(1,128)S(1)}, u32[]{:S(2)}, u32[]{:S(2)}) %collective-permute-start.14) | collective-permute-done | bytes 262176 | tf_op jit(solution)/shard_map/ppermute | solution.py:31
  148.7 6.7 %select_maximum_fusion.5 = f32[2,64,4,10,130]{4,3,2,1,0:T(8,128)S(1)} fusion(f32[2,64,4,1,128]{4,3,2,1,0:T(1,128)S(1)} %collective-permute-done.14, f32[2,64,4,1,128]{4,3,2,1,0:T(1,128)S(1)} %collective-permute-done.13, f32[2,64,1,8,128]{4,3,2,1,0:T(8,128)S(1)} %collective-permute-done.12, f32[2,64,1,8,128]{4,3,2,1,0:T(8,128)S(1)} %collective-permute-done.11, ...), kind=kLoop, calls=%fused_computation.8 | loop fusion | flops 9318400 | bytes 5283840 | tf_op jit(solution)/shard_map/concatenate | solution.py:27
  155.4 1.3 fusion.21
  157.0 8.0 %collective-permute-start.15 = (f32[2,64,1,8,128]{4,3,2,1,0:T(8,128)S(1)}, f32[2,64,1,8,128]{4,3,2,1,0:T(8,128)S(1)}, u32[]{:S(2)}, u32[]{:S(2)}) collective-permute-start(f32[2,64,1,8,128]{4,3,2,1,0:T(8,128)S(1)} %get-tuple-element.31), channel_id=1, source_target_pairs={{0,4},{4,8},{8,12},{12,16},{16,20},{20,24},{24,28},{1,5},{5,9},{9,... | collective-permute-start | bytes 1572872 | tf_op jit(solution)/shard_map/ppermute | solution.py:29
  165.0 1.3 collective-permute-start.16
  166.5 4.1 %collective-permute-done.16 = f32[2,64,1,8,128]{4,3,2,1,0:T(8,128)S(1)} collective-permute-done((f32[2,64,1,8,128]{4,3,2,1,0:T(8,128)S(1)}, f32[2,64,1,8,128]{4,3,2,1,0:T(8,128)S(1)}, u32[]{:S(2)}, u32[]{:S(2)}) %collective-permute-start.16) | collective-permute-done | bytes 524320 | tf_op jit(solution)/shard_map/ppermute | solution.py:31
  170.9 2.5 %collective-permute-start.17 = (f32[2,64,4,1,128]{4,3,2,1,0:T(1,128)S(1)}, f32[2,64,4,1,128]{4,3,2,1,0:T(1,128)S(1)}, u32[]{:S(2)}, u32[]{:S(2)}) collective-permute-start(f32[2,64,4,1,128]{4,3,2,1,0:T(1,128)S(1)} %get-tuple-element.9), channel_id=1, source_target_pairs={{0,1},{1,2},{2,3},{4,5},{5,6},{6,7},{8,9},{9,10},{10,11},{12,13},{... | collective-permute-start | bytes 786440 | tf_op jit(solution)/shard_map/ppermute | solution.py:29
  173.4 1.4 collective-permute-start.18
  174.8 2.4 %collective-permute-done.17 = f32[2,64,4,1,128]{4,3,2,1,0:T(1,128)S(1)} collective-permute-done((f32[2,64,4,1,128]{4,3,2,1,0:T(1,128)S(1)}, f32[2,64,4,1,128]{4,3,2,1,0:T(1,128)S(1)}, u32[]{:S(2)}, u32[]{:S(2)}) %collective-permute-start.17) | collective-permute-done | bytes 262176 | tf_op jit(solution)/shard_map/ppermute | solution.py:29
  177.2 4.6 %collective-permute-done.18 = f32[2,64,4,1,128]{4,3,2,1,0:T(1,128)S(1)} collective-permute-done((f32[2,64,4,1,128]{4,3,2,1,0:T(1,128)S(1)}, f32[2,64,4,1,128]{4,3,2,1,0:T(1,128)S(1)}, u32[]{:S(2)}, u32[]{:S(2)}) %collective-permute-start.18) | collective-permute-done | bytes 262176 | tf_op jit(solution)/shard_map/ppermute | solution.py:31
  181.8 6.7 %select_maximum_fusion = f32[2,64,4,10,130]{4,3,2,1,0:T(8,128)S(1)} fusion(f32[2,64,4,1,128]{4,3,2,1,0:T(1,128)S(1)} %collective-permute-done.18, f32[2,64,4,1,128]{4,3,2,1,0:T(1,128)S(1)} %collective-permute-done.17, f32[2,64,1,8,128]{4,3,2,1,0:T(8,128)S(1)} %collective-permute-done.16, f32[2,64,1,8,128]{4,3,2,1,0:T(8,128)S(1)} %collective-permute-done.15, ...), kind=kLoop, calls=%fused_computation.3 | loop fusion | flops 9318400 | bytes 5283840 | tf_op jit(solution)/shard_map/concatenate | solution.py:27
  188.5 1.3 fusion.14
  192.5 9.5 %all-to-all-start.1 = ((f32[64,2,8,128]{3,2,1,0:T(8,128)}), f32[64,2,8,128]{3,2,1,0:T(8,128)S(1)}, u32[]{:S(2)}, u32[]{:S(2)}) async-start(f32[64,2,8,128]{3,2,1,0:T(8,128)} %bitcast.48), calls=%async_computation.1 | async-start | bytes 1048576 | tf_op jit(solution)/shard_map/all_to_all | solution.py:130
  202.0 9.7 %all-to-all-done.1 = f32[64,2,8,128]{3,2,1,0:T(8,128)S(1)} async-done(((f32[64,2,8,128]{3,2,1,0:T(8,128)}), f32[64,2,8,128]{3,2,1,0:T(8,128)S(1)}, u32[]{:S(2)}, u32[]{:S(2)}) %all-to-all-start.1) | async-done | bytes 524320 | tf_op jit(solution)/shard_map/all_to_all | solution.py:130
  (91 shorter events, 21.3 us)
Async XLA Ops:
  1.2 10.0 %collective-permute-start = (f32[1,16,8,128]{3,1,2,0:T(8,128)S(1)}, f32[1,16,8,128]{3,1,2,0:T(8,128)S(1)}, u32[]{:S(2)}, u32[]{:S(2)}) collective-permute-start(f32[1,16,8,128]{3,1,2,0:T(8,128)S(1)} %slice.399), channel_id=1, source_target_pairs={{4,0},{8,4},{12,8},{16,12},{20,16},{24,20},{28,24},{5,1},{9,5},{13... | collective-permute-start | bytes 196616 | tf_op jit(solution)/shard_map/ppermute | solution.py:18
  9.6 23.3 %copy-start.3 = (f32[8,16,8,128]{3,2,1,0:T(8,128)S(1)}, f32[8,16,8,128]{3,2,1,0:T(8,128)}, u32[]{:S(2)}) copy-start(f32[8,16,8,128]{3,2,1,0:T(8,128)} %param.7) | copy-start | bytes 1572868
  11.1 18.5 %collective-permute-start.1 = (f32[14,16,1,128]{3,1,2,0:T(8,128)S(1)}, f32[14,16,1,128]{3,1,2,0:T(8,128)S(1)}, u32[]{:S(2)}, u32[]{:S(2)}) collective-permute-start(f32[14,16,1,128]{3,1,2,0:T(8,128)S(1)} %get-tuple-element.41), channel_id=1, source_target_pairs={{0,1},{1,2},{2,3},{4,5},{5,6},{6,7},{8,9},{9,10},{10,11},{12,13},{... | collective-permute-start | bytes 344072 | tf_op jit(solution)/shard_map/ppermute | solution.py:29
  16.1 13.5 %collective-permute-start.2 = (f32[14,16,1,128]{3,1,2,0:T(8,128)S(1)}, f32[14,16,1,128]{3,1,2,0:T(8,128)S(1)}, u32[]{:S(2)}, u32[]{:S(2)}) collective-permute-start(f32[14,16,1,128]{3,1,2,0:T(8,128)S(1)} %get-tuple-element.42), channel_id=1, source_target_pairs={{1,0},{2,1},{3,2},{5,4},{6,5},{7,6},{9,8},{10,9},{11,10},{13,12},{... | collective-permute-start | bytes 344072 | tf_op jit(solution)/shard_map/ppermute | solution.py:31
  31.1 1.7 copy-start
  33.9 33.1 %slice-start = ((f32[14,18,10,130]{3,1,2,0:T(8,128)}), f32[6,18,10,130]{3,1,2,0:T(8,128)S(1)}, s32[]{:S(2)}) async-start(f32[14,18,10,130]{3,1,2,0:T(8,128)} %copy-done), calls=%async_computation.2 | async-start | bytes 2949120 | tf_op jit(solution)/shard_map/slice | solution.py:99
  48.8 0.8 copy-start.5
  49.5 0.8 copy-start.7
  50.3 0.8 copy-start.1
  52.2 3.4 %collective-permute-start.3 = (f32[2,64,1,8,128]{4,3,2,1,0:T(8,128)}, f32[2,64,1,8,128]{4,3,2,1,0:T(8,128)}, u32[]{:S(2)}, u32[]{:S(2)}) collective-permute-start(f32[2,64,1,8,128]{4,3,2,1,0:T(8,128)} %get-tuple-element.37), channel_id=1, source_target_pairs={{0,4},{4,8},{8,12},{12,16},{16,20},{20,24},{24,28},{1,5},{5,9},{9,... | collective-permute-start | bytes 1572872 | tf_op jit(solution)/shard_map/ppermute | solution.py:29
  54.3 4.1 %collective-permute-start.4 = (f32[2,64,1,8,128]{4,3,2,1,0:T(8,128)}, f32[2,64,1,8,128]{4,3,2,1,0:T(8,128)}, u32[]{:S(2)}, u32[]{:S(2)}) collective-permute-start(f32[2,64,1,8,128]{4,3,2,1,0:T(8,128)} %get-tuple-element.38), channel_id=1, source_target_pairs={{4,0},{8,4},{12,8},{16,12},{20,16},{24,20},{28,24},{5,1},{9,5},{13... | collective-permute-start | bytes 1572872 | tf_op jit(solution)/shard_map/ppermute | solution.py:31
  61.0 8.7 %collective-permute-start.5 = (f32[2,64,4,1,128]{4,3,2,1,0:T(1,128)}, f32[2,64,4,1,128]{4,3,2,1,0:T(1,128)S(1)}, u32[]{:S(2)}, u32[]{:S(2)}) collective-permute-start(f32[2,64,4,1,128]{4,3,2,1,0:T(1,128)} %get-tuple-element.15), channel_id=1, source_target_pairs={{0,1},{1,2},{2,3},{4,5},{5,6},{6,7},{8,9},{9,10},{10,11},{12,13},{... | collective-permute-start | bytes 786440 | tf_op jit(solution)/shard_map/ppermute | solution.py:29
  65.6 8.6 %collective-permute-start.6 = (f32[2,64,4,1,128]{4,3,2,1,0:T(1,128)}, f32[2,64,4,1,128]{4,3,2,1,0:T(1,128)}, u32[]{:S(2)}, u32[]{:S(2)}) collective-permute-start(f32[2,64,4,1,128]{4,3,2,1,0:T(1,128)} %get-tuple-element.16), channel_id=1, source_target_pairs={{1,0},{2,1},{3,2},{5,4},{6,5},{7,6},{9,8},{10,9},{11,10},{13,12},{... | collective-permute-start | bytes 786440 | tf_op jit(solution)/shard_map/ppermute | solution.py:31
  67.2 16.6 %copy-start.2 = (f32[8,8,16,128]{3,2,1,0:T(8,128)S(1)}, f32[8,8,16,128]{3,2,1,0:T(8,128)}, u32[]{:S(2)}) copy-start(f32[8,8,16,128]{3,2,1,0:T(8,128)} %copy-done.1) | copy-start | bytes 1572868
  84.1 12.2 %collective-permute-start.7 = (f32[2,64,1,8,128]{4,3,2,1,0:T(8,128)S(1)}, f32[2,64,1,8,128]{4,3,2,1,0:T(8,128)S(1)}, u32[]{:S(2)}, u32[]{:S(2)}) collective-permute-start(f32[2,64,1,8,128]{4,3,2,1,0:T(8,128)S(1)} %get-tuple-element.35), channel_id=1, source_target_pairs={{0,4},{4,8},{8,12},{12,16},{16,20},{20,24},{24,28},{1,5},{5,9},{9,... | collective-permute-start | bytes 1572872 | tf_op jit(solution)/shard_map/ppermute | solution.py:29
  94.8 6.7 %collective-permute-start.8 = (f32[2,64,1,8,128]{4,3,2,1,0:T(8,128)S(1)}, f32[2,64,1,8,128]{4,3,2,1,0:T(8,128)S(1)}, u32[]{:S(2)}, u32[]{:S(2)}) collective-permute-start(f32[2,64,1,8,128]{4,3,2,1,0:T(8,128)S(1)} %get-tuple-element.36), channel_id=1, source_target_pairs={{4,0},{8,4},{12,8},{16,12},{20,16},{24,20},{28,24},{5,1},{9,5},{13... | collective-permute-start | bytes 1572872 | tf_op jit(solution)/shard_map/ppermute | solution.py:31
  101.9 7.4 %collective-permute-start.9 = (f32[2,64,4,1,128]{4,3,2,1,0:T(1,128)S(1)}, f32[2,64,4,1,128]{4,3,2,1,0:T(1,128)S(1)}, u32[]{:S(2)}, u32[]{:S(2)}) collective-permute-start(f32[2,64,4,1,128]{4,3,2,1,0:T(1,128)S(1)} %get-tuple-element.13), channel_id=1, source_target_pairs={{0,1},{1,2},{2,3},{4,5},{5,6},{6,7},{8,9},{9,10},{10,11},{12,13},{... | collective-permute-start | bytes 786440 | tf_op jit(solution)/shard_map/ppermute | solution.py:29
  105.4 8.3 %collective-permute-start.10 = (f32[2,64,4,1,128]{4,3,2,1,0:T(1,128)S(1)}, f32[2,64,4,1,128]{4,3,2,1,0:T(1,128)S(1)}, u32[]{:S(2)}, u32[]{:S(2)}) collective-permute-start(f32[2,64,4,1,128]{4,3,2,1,0:T(1,128)S(1)} %get-tuple-element.14), channel_id=1, source_target_pairs={{1,0},{2,1},{3,2},{5,4},{6,5},{7,6},{9,8},{10,9},{11,10},{13,12},{... | collective-permute-start | bytes 786440 | tf_op jit(solution)/shard_map/ppermute | solution.py:31
  122.0 10.5 %collective-permute-start.11 = (f32[2,64,1,8,128]{4,3,2,1,0:T(8,128)S(1)}, f32[2,64,1,8,128]{4,3,2,1,0:T(8,128)S(1)}, u32[]{:S(2)}, u32[]{:S(2)}) collective-permute-start(f32[2,64,1,8,128]{4,3,2,1,0:T(8,128)S(1)} %get-tuple-element.33), channel_id=1, source_target_pairs={{0,4},{4,8},{8,12},{12,16},{16,20},{20,24},{24,28},{1,5},{5,9},{9,... | collective-permute-start | bytes 1572872 | tf_op jit(solution)/shard_map/ppermute | solution.py:29
  131.0 5.6 %collective-permute-start.12 = (f32[2,64,1,8,128]{4,3,2,1,0:T(8,128)S(1)}, f32[2,64,1,8,128]{4,3,2,1,0:T(8,128)S(1)}, u32[]{:S(2)}, u32[]{:S(2)}) collective-permute-start(f32[2,64,1,8,128]{4,3,2,1,0:T(8,128)S(1)} %get-tuple-element.34), channel_id=1, source_target_pairs={{4,0},{8,4},{12,8},{16,12},{20,16},{24,20},{28,24},{5,1},{9,5},{13... | collective-permute-start | bytes 1572872 | tf_op jit(solution)/shard_map/ppermute | solution.py:31
  136.9 7.3 %collective-permute-start.13 = (f32[2,64,4,1,128]{4,3,2,1,0:T(1,128)S(1)}, f32[2,64,4,1,128]{4,3,2,1,0:T(1,128)S(1)}, u32[]{:S(2)}, u32[]{:S(2)}) collective-permute-start(f32[2,64,4,1,128]{4,3,2,1,0:T(1,128)S(1)} %get-tuple-element.11), channel_id=1, source_target_pairs={{0,1},{1,2},{2,3},{4,5},{5,6},{6,7},{8,9},{9,10},{10,11},{12,13},{... | collective-permute-start | bytes 786440 | tf_op jit(solution)/shard_map/ppermute | solution.py:29
  140.4 8.3 %collective-permute-start.14 = (f32[2,64,4,1,128]{4,3,2,1,0:T(1,128)S(1)}, f32[2,64,4,1,128]{4,3,2,1,0:T(1,128)S(1)}, u32[]{:S(2)}, u32[]{:S(2)}) collective-permute-start(f32[2,64,4,1,128]{4,3,2,1,0:T(1,128)S(1)} %get-tuple-element.12), channel_id=1, source_target_pairs={{1,0},{2,1},{3,2},{5,4},{6,5},{7,6},{9,8},{10,9},{11,10},{13,12},{... | collective-permute-start | bytes 786440 | tf_op jit(solution)/shard_map/ppermute | solution.py:31
  157.0 9.5 %collective-permute-start.15 = (f32[2,64,1,8,128]{4,3,2,1,0:T(8,128)S(1)}, f32[2,64,1,8,128]{4,3,2,1,0:T(8,128)S(1)}, u32[]{:S(2)}, u32[]{:S(2)}) collective-permute-start(f32[2,64,1,8,128]{4,3,2,1,0:T(8,128)S(1)} %get-tuple-element.31), channel_id=1, source_target_pairs={{0,4},{4,8},{8,12},{12,16},{16,20},{20,24},{24,28},{1,5},{5,9},{9,... | collective-permute-start | bytes 1572872 | tf_op jit(solution)/shard_map/ppermute | solution.py:29
  165.0 5.5 %collective-permute-start.16 = (f32[2,64,1,8,128]{4,3,2,1,0:T(8,128)S(1)}, f32[2,64,1,8,128]{4,3,2,1,0:T(8,128)S(1)}, u32[]{:S(2)}, u32[]{:S(2)}) collective-permute-start(f32[2,64,1,8,128]{4,3,2,1,0:T(8,128)S(1)} %get-tuple-element.32), channel_id=1, source_target_pairs={{4,0},{8,4},{12,8},{16,12},{20,16},{24,20},{28,24},{5,1},{9,5},{13... | collective-permute-start | bytes 1572872 | tf_op jit(solution)/shard_map/ppermute | solution.py:31
  170.9 6.3 %collective-permute-start.17 = (f32[2,64,4,1,128]{4,3,2,1,0:T(1,128)S(1)}, f32[2,64,4,1,128]{4,3,2,1,0:T(1,128)S(1)}, u32[]{:S(2)}, u32[]{:S(2)}) collective-permute-start(f32[2,64,4,1,128]{4,3,2,1,0:T(1,128)S(1)} %get-tuple-element.9), channel_id=1, source_target_pairs={{0,1},{1,2},{2,3},{4,5},{5,6},{6,7},{8,9},{9,10},{10,11},{12,13},{... | collective-permute-start | bytes 786440 | tf_op jit(solution)/shard_map/ppermute | solution.py:29
  173.4 16.6 %copy-start.8 = (f32[64,2048]{1,0:T(8,128)S(1)}, f32[64,2048]{1,0:T(8,128)}, u32[]{:S(2)}) copy-start(f32[64,2048]{1,0:T(8,128)} %copy-done.7) | copy-start | bytes 1572868
  173.4 8.4 %collective-permute-start.18 = (f32[2,64,4,1,128]{4,3,2,1,0:T(1,128)S(1)}, f32[2,64,4,1,128]{4,3,2,1,0:T(1,128)S(1)}, u32[]{:S(2)}, u32[]{:S(2)}) collective-permute-start(f32[2,64,4,1,128]{4,3,2,1,0:T(1,128)S(1)} %get-tuple-element.10), channel_id=1, source_target_pairs={{1,0},{2,1},{3,2},{5,4},{6,5},{7,6},{9,8},{10,9},{11,10},{13,12},{... | collective-permute-start | bytes 786440 | tf_op jit(solution)/shard_map/ppermute | solution.py:31
  188.5 2.3 %copy-start.6 = (f32[64,2048]{1,0:T(8,128)S(1)}, f32[64,2048]{1,0:T(8,128)}, u32[]{:S(2)}) copy-start(f32[64,2048]{1,0:T(8,128)} %copy-done.5) | copy-start | bytes 1572868
  188.5 23.2 %copy-start.4 = (f32[8,16,8,128]{3,2,1,0:T(8,128)S(1)}, f32[8,16,8,128]{3,2,1,0:T(8,128)}, u32[]{:S(2)}) copy-start(f32[8,16,8,128]{3,2,1,0:T(8,128)} %param.7) | copy-start | bytes 1572868
  192.5 19.2 %all-to-all-start.1 = ((f32[64,2,8,128]{3,2,1,0:T(8,128)}), f32[64,2,8,128]{3,2,1,0:T(8,128)S(1)}, u32[]{:S(2)}, u32[]{:S(2)}) async-start(f32[64,2,8,128]{3,2,1,0:T(8,128)} %bitcast.48), calls=%async_computation.1 | async-start | bytes 1048576 | tf_op jit(solution)/shard_map/all_to_all | solution.py:130
